TPU v7x, 512 devices: a whole 4x4x16 slice. The times are simulated.
512 devices in a mesh: rep: 4 (over y), own: 128 (over x, z, core).
Axes of the slice: x: 4, y: 4, z: 16, core: 2. Of those that a mesh axis runs over, the one named last changes fastest.
Arguments:
- local_weights: bfloat16 [4, 192, 384, 768], P('rep', None, 'own'), may hold values from -6 to 6
- anchor: float32 [256, 384, 768], P('own', 'rep'), may hold values from -6 to 6
- momentum: float32 [256, 384, 768], P('own', 'rep'), may hold values from -6 to 6
- owners: int32 [192], replicated, may hold values from 0 to 127, as said below
Outputs:
- new_weights: float32 [192, 384, 768], P(None, 'own')
- new_momentum: float32 [256, 384, 768], P('own', 'rep')
Inputs may be any that keep to these rules, and one draw needn't show every extreme that they name: Blocks 2i and 2i+1 for i < 48 form one attention projection and have the same owner; different projections have different owners; the 96 embedding blocks that follow go to the owners holding no projection, in runs of consecutive blocks; every owner holds at least one block and at most 2, and some owner holds exactly 2.
All inputs are finite; a program needn't handle non-finite values.
Results may differ from a plain program's by a relative error of at most 0.0003.
Values may be sent and summed in bfloat16 or wider, within the bound.
A program may use at most 64 MiB of HBM per device.

v0:
```python
import jax
import jax.numpy as jnp
from jax import lax
from jax.sharding import PartitionSpec as P

outer_rate = 0.7
momentum_rate = 0.9


def local(local_weights, anchor, momentum, owners):
    n_own = lax.axis_size("own")
    n_rep = lax.axis_size("rep")
    blocks = owners.shape[0]
    stripe = local_weights.shape[2]
    width = local_weights.shape[3]
    slots = anchor.shape[0]
    block_rows = stripe * n_own
    index = jnp.arange(blocks, dtype=jnp.int32)
    same = (owners[None, :] == owners[:, None]) & (index[None, :] < index[:, None])
    slot = jnp.sum(same.astype(jnp.int32), axis=1)
    place = owners * slots + slot
    targets = jnp.arange(n_own * slots, dtype=jnp.int32)
    picker = targets[:, None] == place[None, :]
    source = jnp.sum(jnp.where(picker, index[None, :], 0), axis=1)
    valid = jnp.any(picker, axis=1)
    mine = lax.axis_index("own") * slots + jnp.arange(slots, dtype=jnp.int32)
    live = jnp.any(mine[:, None] == place[None, :], axis=1)
    rows_here = local_weights[0]
    flat = rows_here.reshape(blocks, stripe * width)
    outgoing = jnp.where(
        valid[:, None], jnp.take(flat, source, axis=0), jnp.zeros((), jnp.bfloat16)
    )
    outgoing = outgoing.reshape(n_own, slots, stripe, width)
    arrived = lax.all_to_all(outgoing, "own", split_axis=0, concat_axis=2, tiled=True)
    arrived = arrived.reshape(slots, block_rows, width).astype(jnp.float32)
    total = lax.psum_scatter(arrived, "rep", scatter_dimension=1, tiled=True)
    mean_local = total / n_rep
    outer_grad = anchor - mean_local
    moment = momentum_rate * momentum + outer_grad
    updated = anchor - outer_rate * (outer_grad + momentum_rate * moment)
    alive = live[:, None, None]
    new_momentum = jnp.where(alive, moment, 0.0)
    updated = jnp.where(alive, updated, 0.0)
    whole = lax.all_gather(updated, "rep", axis=1, tiled=True)
    whole = whole.reshape(slots, n_own, stripe, width)
    returned = lax.all_to_all(whole, "own", split_axis=1, concat_axis=0, tiled=True)
    returned = returned.reshape(n_own * slots, stripe * width)
    new_weights = jnp.take(returned, place, axis=0)
    new_weights = new_weights.reshape(blocks, stripe, width)
    return (new_weights, new_momentum)


def solution(mesh):
    return jax.shard_map(
        local,
        mesh=mesh,
        in_specs=(P("rep", None, "own", None), P("own", "rep", None), P("own", "rep", None), P()),
        out_specs=(P(None, "own", None), P("own", "rep", None)),
        check_vma=False,
    )
```

profile of v0, /device:TPU:1, one launch (start us, length us, event | category | flops | bytes accessed | tf_op | source)
XLA Modules:
  0.0 356.4 jit_solution(2367220810949827903)
XLA Ops:
  7.2 0.0 all-reduce.3.cloned.1.call-start
  7.2 0.9 convert_reduce_fusion
  8.1 0.7 compare_and_fusion.1
  8.8 0.1 select_reduce_fusion
  8.9 0.1 fusion.2
  9.1 0.1 reduce_sum.24
  9.2 1.9 copy.26
  11.2 0.1 copy.34
  11.3 1.4 gather_fusion
  12.7 0.6 gather.13
  13.3 0.2 broadcast_in_dim.77
  13.5 1.3 select_select_fusion
  14.8 1.0 copy.27
  15.8 79.9 %all_to_all.24 = bf16[128,2,3,768]{3,1,2,0:T(2,128)(2,1)S(1)} all-to-all(bf16[128,2,3,768]{3,1,2,0:T(2,128)(2,1)S(1)} %copy.27), channel_id=1, replica_groups=mesh['rep'=4,'own'=128] {'own'}, dimensions={0} | all-to-all | bytes 2359296 | tf_op jit(solution)/shard_map/all_to_all | solution.py:34
  95.8 2.2 bitcast_convert_fusion
  98.0 0.0 all-reduce.3.cloned.1.call-update
  98.0 0.0 all-gather.2.cloned.1.call-start
  98.0 1.3 dynamic-slice
  100.1 0.2 compare_reduce_fusion
  100.2 69.7 %all-reduce.3.cloned.1.call-done = f32[2,384,768]{2,0,1:T(2,128)} async-done(((f32[2,384,768]{2,0,1:T(2,128)}), f32[2,384,768]{2,0,1:T(2,128)}) %all-reduce.3.cloned.1.call-update) | async-done | bytes 2359312
  170.0 3.3 broadcast_select_fusion.1
  173.3 0.0 all-gather.2.cloned.1.call-update
  173.3 40.7 %all-gather.2.cloned.1.call-done = f32[2,384,768]{2,0,1:T(2,128)} async-done(((f32[2,96,768]{2,0,1:T(2,128)}), f32[2,384,768]{2,0,1:T(2,128)}) %all-gather.2.cloned.1.call-update) | async-done | bytes 2359312 | tf_op jit(solution)/shard_map/all_gather | solution.py:44
  214.0 16.8 %all-to-all-start.1 = ((f32[2,128,3,768]{3,0,2,1:T(2,128)}), f32[2,128,3,768]{3,0,2,1:T(2,128)S(1)}, u32[]{:S(2)}, u32[]{:S(2)}) async-start(f32[2,128,3,768]{3,0,2,1:T(2,128)} %bitcast.26), calls=%async_computation.1 | async-start | bytes 4718592 | tf_op jit(solution)/shard_map/all_to_all | solution.py:46
  230.8 0.9 copy.33
  231.7 109.2 %all-to-all-done.1 = f32[2,128,3,768]{3,0,2,1:T(2,128)S(1)} async-done(((f32[2,128,3,768]{3,0,2,1:T(2,128)}), f32[2,128,3,768]{3,0,2,1:T(2,128)S(1)}, u32[]{:S(2)}, u32[]{:S(2)}) %all-to-all-start.1) | async-done | bytes 2359328 | tf_op jit(solution)/shard_map/all_to_all | solution.py:46
  340.9 0.8 copy.31
  341.7 0.4 copy.35
  342.1 2.5 gather_fusion.1
  344.6 2.8 gather.15
  347.4 0.6 broadcast_select_fusion
  348.0 1.5 copy.32
  (10 shorter events, 0.1 us)
Async XLA Ops:
  7.2 162.8 %all-reduce.3.cloned.1.call-start = ((), (), s32[]{:S(2)}) async-start(), calls=%async_computation.3 | async-start | bytes 4718592
  98.0 72.0 %copy-start = (f32[2,96,768]{2,1,0:T(8,128)S(1)}, f32[2,96,768]{2,1,0:T(8,128)}, u32[]{:S(2)}) copy-start(f32[2,96,768]{2,1,0:T(8,128)} %param.6) | copy-start | bytes 1769476
  98.0 72.0 %copy-start.1 = (f32[2,96,768]{2,1,0:T(8,128)S(1)}, f32[2,96,768]{2,1,0:T(8,128)}, u32[]{:S(2)}) copy-start(f32[2,96,768]{2,1,0:T(8,128)} %param.5) | copy-start | bytes 1769476
  98.0 116.0 %all-gather.2.cloned.1.call-start = ((), (), s32[]{:S(2)}) async-start(), calls=%async_computation.2 | async-start | bytes 2949120 | tf_op jit(solution)/shard_map/all_gather | solution.py:44
  214.0 126.9 %all-to-all-start.1 = ((f32[2,128,3,768]{3,0,2,1:T(2,128)}), f32[2,128,3,768]{3,0,2,1:T(2,128)S(1)}, u32[]{:S(2)}, u32[]{:S(2)}) async-start(f32[2,128,3,768]{3,0,2,1:T(2,128)} %bitcast.26), calls=%async_computation.1 | async-start | bytes 4718592 | tf_op jit(solution)/shard_map/all_to_all | solution.py:46
Sparse Core Ops, SparseCore 0:
  98.1 71.8 all-reduce.2
  173.5 40.4 all-gather.1
where the time goes:
time: 357 us; the launch traced here: 356 us
  waiting for transfers between devices  220 us (62%)
  blocking collectives  79.9 us (22%)
  starting transfers between devices  16.9 us (5%)
  local copies, waits for them, and re-layouts  15.6 us (4%)
  between operations  14.8 us (4%)
  other arithmetic  9.54 us (3%)
    all_to_all x1, waiting for transfers between devices, local(): lax.all_to_all(whole, 'own', split_axis=1, concat_axis=0, tiled=True)  109 us
    all_to_all x1, blocking collectives, local(): lax.all_to_all(outgoing, 'own', split_axis=0, concat_axis=2, tiled=True)  79.9 us
    unnamed x3, waiting for transfers between devices  69.8 us
    all_gather x1, waiting for transfers between devices, local(): whole = lax.all_gather(updated, 'rep', axis=1, tiled=True)  40.7 us
    all_to_all x1, starting transfers between devices, local(): lax.all_to_all(whole, 'own', split_axis=1, concat_axis=0, tiled=True)  16.8 us
  transfers between devices with their start and end apart: 3, of which 3 were waited for; matrix products, arithmetic and copies ran while one was open for 1% of the time, Pallas kernels for 0%

commit v1 on v0

--- a/solution.py
+++ b/solution.py
@@ -41,7 +41,9 @@
     alive = live[:, None, None]
     new_momentum = jnp.where(alive, moment, 0.0)
     updated = jnp.where(alive, updated, 0.0)
-    whole = lax.all_gather(updated, "rep", axis=1, tiled=True)
+    whole = jnp.concatenate(
+        lax.all_to_all(jnp.stack([updated] * lax.axis_size("rep")), "rep", 0, 0), axis=1
+    )
     whole = whole.reshape(slots, n_own, stripe, width)
     returned = lax.all_to_all(whole, "own", split_axis=1, concat_axis=0, tiled=True)
     returned = returned.reshape(n_own * slots, stripe * width)

time: 357 us -> 348 us (0.975)
  waiting for transfers between devices: 220 us -> 179 us
  blocking collectives: 79.9 us -> 111 us
    all_gather x1 -> x0, waiting for transfers between devices: 40.7 us -> none  [local(): whole = lax.all_gather(updated, 'rep', axis=1, tiled=True)]
    all_to_all x0 -> x1, blocking collectives: none -> 31.4 us  [local(): lax.all_to_all(jnp.stack([updated] * lax.axis_size('rep')), 'rep', 0, 0)]
    unnamed x3 -> x2, waiting for transfers between devices: 69.8 us -> 69.8 us
  transfers between devices with their start and end apart: 3 -> 2, of which waited for: 3 -> 2; matrix products, arithmetic and copies ran while one was open for 1% -> 1% of each run, Pallas kernels for 0% -> 0%
where the time goes in v1:
time: 348 us
  waiting for transfers between devices  179 us (51%)
  blocking collectives  111 us (32%)
  starting transfers between devices  17.9 us (5%)
  local copies, waits for them, and re-layouts  16.2 us (5%)
  between operations  14.8 us (4%)
  other arithmetic  8.72 us (3%)
    all_to_all x1, waiting for transfers between devices, local(): lax.all_to_all(whole, 'own', split_axis=1, concat_axis=0, tiled=True)  109 us
    all_to_all x1, blocking collectives, local(): lax.all_to_all(outgoing, 'own', split_axis=0, concat_axis=2, tiled=True)  79.9 us
    unnamed x2, waiting for transfers between devices  69.8 us
    all_to_all x1, blocking collectives, local(): lax.all_to_all(jnp.stack([updated] * lax.axis_size('rep')), 'rep', 0, 0)  31.4 us
    all_to_all x1, starting transfers between devices, local(): lax.all_to_all(whole, 'own', split_axis=1, concat_axis=0, tiled=True)  17.9 us
  transfers between devices with their start and end apart: 2, of which 2 were waited for; matrix products, arithmetic and copies ran while one was open for 1% of the time, Pallas kernels for 0%

profile of v1, /device:TPU:1, one launch (start us, length us, event | category | flops | bytes accessed | tf_op | source)
XLA Modules:
  0.0 348.0 jit_solution(1530592718284688268)
XLA Ops:
  7.2 0.0 all-reduce.3.cloned.1.call-start
  7.2 0.9 convert_reduce_fusion
  8.1 0.7 compare_and_fusion.1
  8.8 0.1 select_reduce_fusion
  8.9 0.1 fusion.2
  9.1 0.1 reduce_sum.24
  9.2 1.9 copy.25
  11.2 0.1 copy.33
  11.3 1.4 gather_fusion
  12.7 0.6 gather.13
  13.3 0.2 broadcast_in_dim.77
  13.5 1.3 select_select_fusion
  14.8 1.0 copy.26
  15.8 79.9 %all_to_all.29 = bf16[128,2,3,768]{3,1,2,0:T(2,128)(2,1)S(1)} all-to-all(bf16[128,2,3,768]{3,1,2,0:T(2,128)(2,1)S(1)} %copy.26), channel_id=1, replica_groups=mesh['rep'=4,'own'=128] {'own'}, dimensions={0} | all-to-all | bytes 2359296 | tf_op jit(solution)/shard_map/all_to_all | solution.py:34
  95.8 2.2 bitcast_convert_fusion
  98.0 0.0 all-reduce.3.cloned.1.call-update
  98.0 1.4 dynamic-slice
  100.0 0.2 compare_reduce_fusion
  100.2 69.8 %all-reduce.3.cloned.1.call-done = f32[2,384,768]{2,0,1:T(2,128)} async-done(((f32[2,384,768]{2,0,1:T(2,128)}), f32[2,384,768]{2,0,1:T(2,128)}) %all-reduce.3.cloned.1.call-update) | async-done | bytes 2359312
  170.0 0.0 copy-done
  170.0 2.5 broadcast_select_fusion.1
  172.5 0.6 stack.2
  173.1 31.4 %all_to_all.30 = f32[4,2,96,768]{3,1,2,0:T(2,128)} all-to-all(f32[4,2,96,768]{3,1,2,0:T(2,128)S(1)} %stack.2), channel_id=1, replica_groups=mesh['rep'=4,'own'=128] {'rep'}, dimensions={0} | all-to-all | bytes 4718592 | tf_op jit(solution)/shard_map/all_to_all | solution.py:45
  204.5 17.9 %all-to-all-start.2 = ((f32[2,128,3,768]{3,0,2,1:T(2,128)}), f32[2,128,3,768]{3,0,2,1:T(2,128)S(1)}, u32[]{:S(2)}, u32[]{:S(2)}) async-start(f32[2,128,3,768]{3,0,2,1:T(2,128)} %bitcast.7), calls=%async_computation.2 | async-start | bytes 4718592 | tf_op jit(solution)/shard_map/all_to_all | solution.py:48
  222.4 0.9 copy.32
  223.3 109.2 %all-to-all-done.2 = f32[2,128,3,768]{3,0,2,1:T(2,128)S(1)} async-done(((f32[2,128,3,768]{3,0,2,1:T(2,128)}), f32[2,128,3,768]{3,0,2,1:T(2,128)S(1)}, u32[]{:S(2)}, u32[]{:S(2)}) %all-to-all-start.2) | async-done | bytes 2359328 | tf_op jit(solution)/shard_map/all_to_all | solution.py:48
  332.5 0.8 copy.30
  333.3 0.4 copy.34
  333.7 2.5 gather_fusion.1
  336.2 2.8 gather.15
  339.0 0.6 broadcast_select_fusion
  339.6 1.5 copy.31
  (9 shorter events, 0.1 us)
Async XLA Ops:
  7.2 162.8 %all-reduce.3.cloned.1.call-start = ((), (), s32[]{:S(2)}) async-start(), calls=%async_computation.3 | async-start | bytes 4718592
  98.0 72.0 %copy-start = (f32[2,96,768]{2,1,0:T(8,128)S(1)}, f32[2,96,768]{2,1,0:T(8,128)}, u32[]{:S(2)}) copy-start(f32[2,96,768]{2,1,0:T(8,128)} %param.6) | copy-start | bytes 1769476
  98.0 72.0 %copy-start.1 = (f32[2,96,768]{2,1,0:T(8,128)S(1)}, f32[2,96,768]{2,1,0:T(8,128)}, u32[]{:S(2)}) copy-start(f32[2,96,768]{2,1,0:T(8,128)} %param.5) | copy-start | bytes 1769476
  204.5 127.9 %all-to-all-start.2 = ((f32[2,128,3,768]{3,0,2,1:T(2,128)}), f32[2,128,3,768]{3,0,2,1:T(2,128)S(1)}, u32[]{:S(2)}, u32[]{:S(2)}) async-start(f32[2,128,3,768]{3,0,2,1:T(2,128)} %bitcast.7), calls=%async_computation.2 | async-start | bytes 4718592 | tf_op jit(solution)/shard_map/all_to_all | solution.py:48
Sparse Core Ops, SparseCore 0:
  98.1 71.8 all-reduce.2
